TPU v7x, 32 devices: a whole 2x2x4 slice. The times are simulated.
32 devices in a mesh: tensor: 2 (over y), dp: 16 (over z, x, core).
Axes of the slice: x: 2, y: 2, z: 4, core: 2. Of those that a mesh axis runs over, the one named last changes fastest.
Arguments:
- inputs: bfloat16 [2, 4096, 768], P(None, 'dp'), may hold values from -6 to 6
- cotangent: bfloat16 [2, 4096, 768], P(None, 'dp'), may hold values from -6 to 6
- segments: int32 [2, 4096], replicated, may hold values from 0 to 31, never falling along the last dimension, each value on 1 to 512 neighbouring positions
- qkv_weight: float32 [768, 3, 768], P('dp', None, 'tensor'), may hold values from -0.21875 to 0.21875
- out_weight: float32 [768, 768], P('dp', 'tensor'), may hold values from -0.875 to 0.875
- gateup_weight: float32 [768, 2, 3072], P('dp', None, 'tensor'), may hold values from -0.21875 to 0.21875
- down_weight: float32 [768, 3072], P('dp', 'tensor'), may hold values from -0.21875 to 0.21875
- norm_gains: float32 [768, 2], P('dp'), may hold values from 0.5 to 1.5
- qkv_momentum: float32 [768, 3, 768], P('dp', None, 'tensor'), may hold values from -64 to 64
- out_momentum: float32 [768, 768], P('dp', 'tensor'), may hold values from -64 to 64
- gateup_momentum: float32 [768, 2, 3072], P('dp', None, 'tensor'), may hold values from -64 to 64
- down_momentum: float32 [768, 3072], P('dp', 'tensor'), may hold values from -64 to 64
- gains_momentum: float32 [768, 2], P('dp'), may hold values from -64 to 64
- qkv_average: float32 [768, 3, 768], P('dp', None, 'tensor'), may hold values from -0.21875 to 0.21875
- out_average: float32 [768, 768], P('dp', 'tensor'), may hold values from -0.875 to 0.875
- gateup_average: float32 [768, 2, 3072], P('dp', None, 'tensor'), may hold values from -0.21875 to 0.21875
- down_average: float32 [768, 3072], P('dp', 'tensor'), may hold values from -0.21875 to 0.21875
- gains_average: float32 [768, 2], P('dp'), may hold values from -0.5 to 0.5
Outputs:
- output: bfloat16 [2, 4096, 768], P(None, 'dp')
- input_grad: float32 [2, 4096, 768], P(None, 'dp')
- qkv_grad: float32 [768, 3, 768], P('dp', None, 'tensor')
- out_grad: float32 [768, 768], P('dp', 'tensor')
- gateup_grad: float32 [768, 2, 3072], P('dp', None, 'tensor')
- down_grad: float32 [768, 3072], P('dp', 'tensor')
- gains_grad: float32 [768, 2], P('dp')
- qkv_moment: float32 [768, 3, 768], P('dp', None, 'tensor')
- out_moment: float32 [768, 768], P('dp', 'tensor')
- gateup_moment: float32 [768, 2, 3072], P('dp', None, 'tensor')
- down_moment: float32 [768, 3072], P('dp', 'tensor')
- gains_moment: float32 [768, 2], P('dp')
- qkv_updated: float32 [768, 3, 768], P('dp', None, 'tensor')
- out_updated: float32 [768, 768], P('dp', 'tensor')
- gateup_updated: float32 [768, 2, 3072], P('dp', None, 'tensor')
- down_updated: float32 [768, 3072], P('dp', 'tensor')
- gains_updated: float32 [768, 2], P('dp')
- qkv_averaged: float32 [768, 3, 768], P('dp', None, 'tensor')
- out_averaged: float32 [768, 768], P('dp', 'tensor')
- gateup_averaged: float32 [768, 2, 3072], P('dp', None, 'tensor')
- down_averaged: float32 [768, 3072], P('dp', 'tensor')
- gains_averaged: float32 [768, 2], P('dp')
Inputs may be any that keep to these rules, and one draw needn't show every extreme that they name: `segments`: along each sequence the document numbers never fall; every document has 1 to 512 tokens and one document of each sequence has exactly 512.
All inputs are finite; a program needn't handle non-finite values.
Results may differ from a plain program's by a relative error of at most 0.015.
The roundings to bfloat16 on the way count: a program that leaves them out, or rounds other values in their place, can miss the bound.
Values may be sent and summed in bfloat16 or wider, within the bound.
No kernel may reach another device: no remote copies, remote signals or barrier semaphores. Data moves between devices by JAX's collectives and lax.ppermute only.
A program may use at most 128 MiB of HBM per device.

v0:
```python
import jax
import jax.numpy as jnp
from jax import lax
from jax.sharding import PartitionSpec as P

HEAD_DIM = 64
REACH = 2
NORM_EPS = 1e-05
ROPE_BASE = 10000.0
MOMENTUM = 0.9
LEARN_RATE = 0.0003
AVERAGE_RATE = 0.9
MASKED = -1e30


def from_behind(value, axis, steps):
    count = lax.axis_size(axis)
    initial, last = (max(0, -steps), min(count, count - steps))
    return lax.ppermute(value, axis, [(source, source + steps) for source in range(initial, last)])


def rotate_half(values):
    half = values.shape[-1] // 2
    return jnp.concatenate([-values[..., half:], values[..., :half]], axis=-1)


def rope_tables(first, count):
    position = (first + jnp.arange(count, dtype=jnp.int32)).astype(jnp.float32)
    inverse = ROPE_BASE ** (-jnp.arange(0, HEAD_DIM, 2, dtype=jnp.float32) / HEAD_DIM)
    angles = position[:, None] * inverse[None, :]
    angles = jnp.concatenate([angles, angles], axis=-1)
    return (jnp.cos(angles)[:, None, :], jnp.sin(angles)[:, None, :])


def apply_rope(values, cosine, sine):
    return values * cosine + rotate_half(values) * sine


def undo_rope(gradient, cosine, sine):
    return gradient * cosine - rotate_half(gradient * sine)


def norm_forward(values, gain):
    scale_inv = lax.rsqrt(jnp.mean(values * values, axis=-1, keepdims=True) + NORM_EPS)
    unit = values * scale_inv
    return (scale_inv, unit, (unit * gain).astype(jnp.bfloat16))


def norm_backward(scale_inv, unit, gain, upstream):
    weighted = upstream * gain
    inner = jnp.mean(weighted * unit, axis=-1, keepdims=True)
    return (scale_inv * (weighted - unit * inner), jnp.sum(unit * upstream, axis=0))


def scores_of(queries, keys_all, visible):
    raw = jnp.einsum("qhe,khe->hqk", queries, keys_all, preferred_element_type=jnp.float32)
    return jnp.where(visible[None], raw * HEAD_DIM ** (-0.5), MASKED)


def micro_step(tokens, upstream, seg_row, whole, rank):
    qkv_full, out_full, gateup_full, down_full, gains_full = whole
    gain_one = gains_full[:, 0].astype(jnp.float32)
    gain_two = gains_full[:, 1].astype(jnp.float32)
    count = tokens.shape[0]
    width = qkv_full.shape[2]
    heads = width // HEAD_DIM
    span = (REACH + 1) * count
    start = rank * count
    scale = HEAD_DIM ** (-0.5)
    tokens_wide = tokens.astype(jnp.float32)
    scale_one, unit_one, normed_one = norm_forward(tokens_wide, gain_one)
    mixed = jnp.einsum("td,dch->tch", normed_one, qkv_full, preferred_element_type=jnp.float32)
    cosine, sine = rope_tables(start, count)
    queries = apply_rope(mixed[:, 0].reshape(count, heads, HEAD_DIM), cosine, sine).astype(
        jnp.bfloat16
    )
    keys_own = apply_rope(mixed[:, 1].reshape(count, heads, HEAD_DIM), cosine, sine).astype(
        jnp.bfloat16
    )
    values_own = mixed[:, 2].reshape(count, heads, HEAD_DIM).astype(jnp.bfloat16)
    earlier = []
    for hop in range(REACH, 0, -1):
        earlier.append(from_behind((keys_own, values_own), "dp", hop))
    keys_all = jnp.concatenate([received[0] for received in earlier] + [keys_own], axis=0)
    values_all = jnp.concatenate([received[1] for received in earlier] + [values_own], axis=0)
    padded = jnp.concatenate([jnp.full((REACH * count,), -1, jnp.int32), seg_row])
    seg_keys = lax.dynamic_slice_in_dim(padded, start, span)
    seg_query = lax.dynamic_slice_in_dim(seg_row, start, count)
    query_pos = jnp.arange(count, dtype=jnp.int32)[:, None] + REACH * count
    key_pos = jnp.arange(span, dtype=jnp.int32)[None, :]
    visible = (seg_query[:, None] == seg_keys[None, :]) & (key_pos <= query_pos)
    scores = scores_of(queries, keys_all, visible)
    peak = jnp.max(scores, axis=-1, keepdims=True)
    expon = jnp.exp(scores - peak)
    totals = jnp.sum(expon, axis=-1, keepdims=True)
    log_total = peak + jnp.log(totals)
    probs_low = (expon / totals).astype(jnp.bfloat16)
    attended = jnp.einsum("hqk,khe->qhe", probs_low, values_all, preferred_element_type=jnp.float32)
    attended = attended.reshape(count, width).astype(jnp.bfloat16)
    branch = jnp.einsum("th,dh->td", attended, out_full, preferred_element_type=jnp.float32)
    branch = lax.psum(branch, "tensor")
    resid = tokens_wide + branch
    scale_two, unit_two, normed_two = norm_forward(resid, gain_two)
    gateup = jnp.einsum("td,dcf->tcf", normed_two, gateup_full, preferred_element_type=jnp.float32)
    gate = gateup[:, 0]
    upward = gateup[:, 1]
    sigma = jax.nn.sigmoid(gate)
    active = gate * sigma
    hidden = (active * upward).astype(jnp.bfloat16)
    down_part = jnp.einsum("tf,df->td", hidden, down_full, preferred_element_type=jnp.float32)
    down_part = lax.psum(down_part.astype(jnp.bfloat16), "tensor").astype(jnp.float32)
    result = (resid + down_part).astype(jnp.bfloat16)
    grad_hidden = jnp.einsum("td,df->tf", upstream, down_full, preferred_element_type=jnp.float32)
    down_grad = jnp.einsum("td,tf->df", upstream, hidden, preferred_element_type=jnp.float32)
    grad_gate = grad_hidden * upward * sigma * (1.0 + gate * (1.0 - sigma))
    grad_up = grad_hidden * active
    grad_gateup = jnp.stack([grad_gate, grad_up], axis=1).astype(jnp.bfloat16)
    gateup_grad = jnp.einsum(
        "td,tcf->dcf", normed_two, grad_gateup, preferred_element_type=jnp.float32
    )
    grad_normed_two = jnp.einsum(
        "tcf,dcf->td", grad_gateup, gateup_full, preferred_element_type=jnp.float32
    )
    grad_normed_two = lax.psum(grad_normed_two, "tensor")
    grad_resid_norm, gain_two_grad = norm_backward(scale_two, unit_two, gain_two, grad_normed_two)
    grad_resid = upstream.astype(jnp.float32) + grad_resid_norm
    grad_branch = grad_resid.astype(jnp.bfloat16)
    grad_attended = jnp.einsum(
        "td,dh->th", grad_branch, out_full, preferred_element_type=jnp.float32
    ).astype(jnp.bfloat16)
    out_grad = jnp.einsum("td,th->dh", grad_branch, attended, preferred_element_type=jnp.float32)
    grad_heads = grad_attended.reshape(count, heads, HEAD_DIM)
    scores = scores_of(queries, keys_all, visible)
    probs = jnp.exp(scores - log_total)
    probs_back = probs.astype(jnp.bfloat16)
    grad_probs = jnp.einsum(
        "qhe,khe->hqk", grad_heads, values_all, preferred_element_type=jnp.float32
    )
    inner = jnp.sum(probs * grad_probs, axis=-1, keepdims=True)
    grad_scores = (probs * (grad_probs - inner)).astype(jnp.bfloat16)
    grad_queries = (
        jnp.einsum("hqk,khe->qhe", grad_scores, keys_all, preferred_element_type=jnp.float32)
        * scale
    )
    grad_keys = (
        jnp.einsum("hqk,qhe->khe", grad_scores, queries, preferred_element_type=jnp.float32) * scale
    )
    grad_values = jnp.einsum(
        "hqk,qhe->khe", probs_back, grad_heads, preferred_element_type=jnp.float32
    )
    own_keys = grad_keys[REACH * count :]
    own_values = grad_values[REACH * count :]
    for hop in range(1, REACH + 1):
        first = (REACH - hop) * count
        returned = (
            from_behind(grad_keys[first : first + count].astype(jnp.bfloat16), "dp", -hop).astype(
                jnp.float32
            ),
            from_behind(grad_values[first : first + count].astype(jnp.bfloat16), "dp", -hop).astype(
                jnp.float32
            ),
        )
        own_keys = own_keys + returned[0]
        own_values = own_values + returned[1]
    grad_q = undo_rope(grad_queries, cosine, sine).reshape(count, width)
    grad_k = undo_rope(own_keys, cosine, sine).reshape(count, width)
    grad_v = own_values.reshape(count, width)
    grad_mixed = jnp.stack([grad_q, grad_k, grad_v], axis=1).astype(jnp.bfloat16)
    qkv_grad = jnp.einsum("td,tch->dch", normed_one, grad_mixed, preferred_element_type=jnp.float32)
    grad_normed_one = jnp.einsum(
        "tch,dch->td", grad_mixed, qkv_full, preferred_element_type=jnp.float32
    )
    grad_normed_one = lax.psum(grad_normed_one, "tensor")
    grad_tokens_norm, gain_one_grad = norm_backward(scale_one, unit_one, gain_one, grad_normed_one)
    grad_tokens = grad_resid + grad_tokens_norm
    gains_grad = jnp.stack([gain_one_grad, gain_two_grad], axis=1)
    return (result, grad_tokens, (qkv_grad, out_grad, gateup_grad, down_grad, gains_grad))


def body(
    inputs,
    cotangent,
    segments,
    qkv_weight,
    out_weight,
    gateup_weight,
    down_weight,
    norm_gains,
    qkv_momentum,
    out_momentum,
    gateup_momentum,
    down_momentum,
    gains_momentum,
    qkv_average,
    out_average,
    gateup_average,
    down_average,
    gains_average,
):
    masters = (qkv_weight, out_weight, gateup_weight, down_weight, norm_gains)
    shards = tuple((master.astype(jnp.bfloat16) for master in masters))
    rank = lax.axis_index("dp")
    totals = tuple((jnp.zeros(master.shape, jnp.float32) for master in masters))
    results = []
    input_grads = []
    for index in range(inputs.shape[0]):
        whole = (
            lax.all_gather(shards[0], "dp", axis=0, tiled=True),
            lax.all_gather(shards[1], "dp", axis=0, tiled=True),
            lax.all_gather(shards[2], "dp", axis=0, tiled=True),
            lax.all_gather(shards[3], "dp", axis=0, tiled=True),
            lax.all_gather(shards[4], "dp", axis=0, tiled=True),
        )
        result, grad_tokens, local_grads = micro_step(
            inputs[index], cotangent[index], segments[index], whole, rank
        )
        shared = (
            lax.psum_scatter(local_grads[0], "dp", scatter_dimension=0, tiled=True),
            lax.psum_scatter(local_grads[1], "dp", scatter_dimension=0, tiled=True),
            lax.psum_scatter(local_grads[2], "dp", scatter_dimension=0, tiled=True),
            lax.psum_scatter(local_grads[3], "dp", scatter_dimension=0, tiled=True),
            lax.psum_scatter(local_grads[4], "dp", scatter_dimension=0, tiled=True),
        )
        totals = tuple((total + piece for total, piece in zip(totals, shared)))
        results.append(result)
        input_grads.append(grad_tokens)
    moments = (qkv_momentum, out_momentum, gateup_momentum, down_momentum, gains_momentum)
    averages = (qkv_average, out_average, gateup_average, down_average, gains_average)
    new_moments = tuple(
        (MOMENTUM * previous + gradient for previous, gradient in zip(moments, totals))
    )
    updated = tuple(
        (
            master - LEARN_RATE * (gradient + MOMENTUM * moment)
            for master, gradient, moment in zip(masters, totals, new_moments)
        )
    )
    averaged = tuple(
        (
            AVERAGE_RATE * previous + (1.0 - AVERAGE_RATE) * weight
            for previous, weight in zip(averages, updated)
        )
    )
    return (
        (jnp.stack(results), jnp.stack(input_grads))
        + tuple(totals)
        + new_moments
        + updated
        + averaged
    )


def solution(mesh):
    return jax.shard_map(
        body,
        mesh=mesh,
        in_specs=(
            P(None, "dp", None),
            P(None, "dp", None),
            P(),
            P("dp", None, "tensor"),
            P("dp", "tensor"),
            P("dp", None, "tensor"),
            P("dp", "tensor"),
            P("dp", None),
            P("dp", None, "tensor"),
            P("dp", "tensor"),
            P("dp", None, "tensor"),
            P("dp", "tensor"),
            P("dp", None),
            P("dp", None, "tensor"),
            P("dp", "tensor"),
            P("dp", None, "tensor"),
            P("dp", "tensor"),
            P("dp", None),
        ),
        out_specs=(
            P(None, "dp", None),
            P(None, "dp", None),
            P("dp", None, "tensor"),
            P("dp", "tensor"),
            P("dp", None, "tensor"),
            P("dp", "tensor"),
            P("dp", None),
            P("dp", None, "tensor"),
            P("dp", "tensor"),
            P("dp", None, "tensor"),
            P("dp", "tensor"),
            P("dp", None),
            P("dp", None, "tensor"),
            P("dp", "tensor"),
            P("dp", None, "tensor"),
            P("dp", "tensor"),
            P("dp", None),
            P("dp", None, "tensor"),
            P("dp", "tensor"),
            P("dp", None, "tensor"),
            P("dp", "tensor"),
            P("dp", None),
        ),
        check_vma=False,
    )
```

profile of v0, /device:TPU:0, one launch (start us, length us, event | category | flops | bytes accessed | tf_op | source)
XLA Modules:
  0.0 908.0 jit_solution(874168385717380845)
XLA Ops:
  9.7 23.1 %all-gather = bf16[16,48,2]{1,2,0:T(2,128)(2,1)S(1)} all-gather(bf16[1,48,2]{1,2,0:T(2,128)(2,1)S(1)} %convert_bitcast_fusion), channel_id=1, replica_groups=mesh['tensor'=2,'dp'=16] {'dp'}, dimensions={0}, use_global_device_ids=true | all-gather | bytes 3264 | tf_op jit(solution)/shard_map/all_gather | solution.py:212
  37.1 21.0 %all_gather.22 = bf16[768,384]{1,0:T(8,128)(2,1)S(1)} all-gather(bf16[48,384]{1,0:T(8,128)(2,1)S(1)} %convert_element_type.228), channel_id=1, replica_groups=mesh['tensor'=2,'dp'=16] {'dp'}, dimensions={0}, use_global_device_ids=true | all-gather | bytes 626688 | tf_op jit(solution)/shard_map/all_gather | solution.py:209
  58.1 2.2 fusion.152
  64.1 2.2 fusion.149
  68.3 1.9 copy.154
  74.3 2.4 fusion.91
  76.7 3.1 collective-permute-start.7
  79.8 2.8 collective-permute-start.6
  85.5 2.2 collective-permute-start.4
  88.9 1.9 collective-permute-start.3
  92.7 2.3 collective-permute-start.1
  95.0 2.3 fusion.161
  98.7 5.4 collective-permute-start
  106.6 2.5 fusion.44
  114.4 49.1 %all-reduce.15.cloned.1.call-done = (f32[256,768]{1,0:T(8,128)}, f32[256,768]{1,0:T(8,128)}) async-done(((f32[256,768]{1,0:T(8,128)}, f32[256,768]{1,0:T(8,128)}), (f32[256,768]{1,0:T(8,128)}, f32[256,768]{1,0:T(8,128)})) %all-reduce.15.cloned.1.call-update) | async-done | bytes 1572880 | tf_op jit(solution)/shard_map/psum | solution.py:101
  165.2 54.3 %all-gather.7.cloned.1.call-done = bf16[768,2,1536]{2,0,1:T(8,128)(2,1)} async-done(((bf16[48,2,1536]{2,0,1:T(8,128)(2,1)}), bf16[768,2,1536]{2,0,1:T(8,128)(2,1)}) %all-gather.7.cloned.1.call-update) | async-done | bytes 4718608 | tf_op jit(solution)/shard_map/all_gather | solution.py:210
  219.6 3.9 fusion.124
  228.3 3.2 add_bitcast_fusion
  231.5 6.1 copy.189
  237.7 74.3 %reduce-scatter.16.cloned.1.call-done = f32[48,1536]{1,0:T(8,128)} async-done(((f32[768,1536]{1,0:T(8,128)}), f32[48,1536]{1,0:T(8,128)}) %reduce-scatter.16.cloned.1.call-update) | async-done | bytes 294928
  312.0 2.3 multiply_add_fusion.2
  314.5 41.7 %all-gather.9.cloned.1.call-done = bf16[768,1536]{1,0:T(8,128)(2,1)} async-done(((bf16[48,1536]{1,0:T(8,128)(2,1)}), bf16[768,1536]{1,0:T(8,128)(2,1)}) %all-gather.9.cloned.1.call-update) | async-done | bytes 2359312 | tf_op jit(solution)/shard_map/all_gather | solution.py:211
  356.2 3.9 fusion.73
  362.7 2.3 convolution_bitcast_fusion.1
  365.0 2.3 convolution_bitcast_fusion
  367.5 4.5 convolution_convert_fusion
  373.8 44.0 %all-reduce.13.cloned.1.call-done = (f32[256,768]{1,0:T(8,128)}, f32[256,768]{1,0:T(8,128)}) async-done(((f32[256,768]{1,0:T(8,128)}, f32[256,768]{1,0:T(8,128)}), (f32[256,768]{1,0:T(8,128)}, f32[256,768]{1,0:T(8,128)})) %all-reduce.13.cloned.1.call-update) | async-done | bytes 1572880 | tf_op jit(solution)/shard_map/psum | solution.py:124
  417.8 2.4 multiply_reduce_fusion.3
  420.2 35.5 %all-reduce.17.cloned.1.call-done = (bf16[256,768]{1,0:T(8,128)(2,1)}, bf16[256,768]{1,0:T(8,128)(2,1)}) async-done(((bf16[256,768]{1,0:T(8,128)(2,1)}, bf16[256,768]{1,0:T(8,128)(2,1)}), (bf16[256,768]{1,0:T(8,128)(2,1)}, bf16[256,768]{1,0:T(8,128)(2,1)})) %all-reduce.17.cloned.1.call-update) | async-done | bytes 786448 | tf_op jit(solution)/shard_map/psum | solution.py:111
  455.7 3.2 multiply_add_fusion.1
  463.3 4.5 fusion.166
  471.2 4.3 fusion.163
  478.9 2.4 multiply_reduce_fusion
  490.0 2.0 convolution_bitcast_fusion.4
  511.8 7.5 collective-permute-done.9
  520.8 2.3 fusion.97
  526.7 3.4 convolution_bitcast_fusion.2
  536.7 3.6 fusion.110
  540.3 47.0 %all-reduce.11.cloned.1.call-done = (f32[256,768]{1,0:T(8,128)}, f32[256,768]{1,0:T(8,128)}) async-done(((f32[256,768]{1,0:T(8,128)}, f32[256,768]{1,0:T(8,128)}), (f32[256,768]{1,0:T(8,128)}, f32[256,768]{1,0:T(8,128)})) %all-reduce.11.cloned.1.call-update) | async-done | bytes 1572880 | tf_op jit(solution)/shard_map/psum | solution.py:173
  587.4 2.5 fusion.53
  592.2 4.8 convolution_add_fusion.1
  597.7 3.0 fusion.46
  600.7 5.2 convolution_add_fusion
  607.0 2.0 pad_maximum_fusion.7
  612.6 37.2 %reduce-scatter.12.cloned.1.call-done = f32[48,384]{1,0:T(8,128)} async-done(((f32[768,384]{1,0:T(8,128)}), f32[48,384]{1,0:T(8,128)}) %reduce-scatter.12.cloned.1.call-update) | async-done | bytes 73744 | tf_op jit(solution)/shard_map/reduce_scatter | solution.py:219
  651.4 57.3 %reduce-scatter.18.cloned.1.call-done = f32[48,2]{1,0:T(8,128)} async-done(((f32[768,2]{1,0:T(8,128)}), f32[48,2]{1,0:T(8,128)}) %reduce-scatter.18.cloned.1.call-update) | async-done | bytes 400
  710.1 70.2 %reduce-scatter.10.cloned.1.call-done = f32[48,3,384]{2,0,1:T(8,128)} async-done(((f32[768,3,384]{2,0,1:T(8,128)}), f32[48,3,384]{2,0,1:T(8,128)}) %reduce-scatter.10.cloned.1.call-update) | async-done | bytes 221200 | tf_op jit(solution)/shard_map/reduce_scatter | solution.py:218
  782.2 112.1 %reduce-scatter.14.cloned.1.call-done = f32[48,2,1536]{2,0,1:T(8,128)} async-done(((f32[768,2,1536]{2,0,1:T(8,128)}), f32[48,2,1536]{2,0,1:T(8,128)}) %reduce-scatter.14.cloned.1.call-update) | async-done | bytes 589840 | tf_op jit(solution)/shard_map/reduce_scatter | solution.py:220
  (354 shorter events, 112.1 us)
Async XLA Ops:
  7.2 50.9 %copy-start.2 = (bf16[2,256,768]{2,1,0:T(8,128)(2,1)S(1)}, bf16[2,256,768]{2,1,0:T(8,128)(2,1)}, u32[]{:S(2)}) copy-start(bf16[2,256,768]{2,1,0:T(8,128)(2,1)} %param.18) | copy-start | bytes 2359300
  7.2 50.9 %all-gather.5.cloned.1.call-start = ((), (), s32[]{:S(2)}) async-start(), calls=%async_computation.5 | async-start | bytes 1880064 | tf_op jit(solution)/shard_map/all_gather | solution.py:208
  8.9 154.6 %all-reduce.15.cloned.1.call-start = ((), (), s32[]{:S(2)}) async-start(), calls=%async_computation.15 | async-start | bytes 3145728 | tf_op jit(solution)/shard_map/psum | solution.py:101
  35.6 38.6 %copy-start.51 = (f32[256,64]{0,1:T(8,128)}, f32[256,64]{0,1:T(8,128)S(1)}, u32[]{:S(2)}) copy-start(f32[256,64]{0,1:T(8,128)S(1)} %get-tuple-element.207) | copy-start | bytes 196612
  35.6 38.6 %copy-start.53 = (f32[256,64]{0,1:T(8,128)}, f32[256,64]{0,1:T(8,128)S(1)}, u32[]{:S(2)}) copy-start(f32[256,64]{0,1:T(8,128)S(1)} %get-tuple-element.206) | copy-start | bytes 196612
  76.7 14.2 %collective-permute-start.7 = (bf16[256,6,64]{0,2,1:T(8,128)(2,1)}, bf16[256,6,64]{0,2,1:T(8,128)(2,1)}, u32[]{:S(2)}, u32[]{:S(2)}) collective-permute-start(bf16[256,6,64]{0,2,1:T(8,128)(2,1)} %get-tuple-element.194), channel_id=1, source_target_pairs={{0,1},{1,2},{2,3},{3,4},{4,5},{5,6},{6,7},{7,8},{8,9},{9,10},{10,1... | collective-permute-start | bytes 589832 | tf_op jit(solution)/shard_map/ppermute | solution.py:19
  79.8 12.9 %collective-permute-start.6 = (bf16[256,6,64]{0,2,1:T(8,128)(2,1)}, bf16[256,6,64]{0,2,1:T(8,128)(2,1)}, u32[]{:S(2)}, u32[]{:S(2)}) collective-permute-start(bf16[256,6,64]{0,2,1:T(8,128)(2,1)} %get-tuple-element.194), channel_id=1, source_target_pairs={{0,2},{1,3},{2,4},{3,5},{4,6},{5,7},{6,8},{7,9},{8,10},{9,11},{10,... | collective-permute-start | bytes 589832 | tf_op jit(solution)/shard_map/ppermute | solution.py:19
  83.9 22.6 %collective-permute-start.5 = (bf16[256,6,64]{0,2,1:T(8,128)(2,1)S(1)}, bf16[256,6,64]{0,2,1:T(8,128)(2,1)S(1)}, u32[]{:S(2)}, u32[]{:S(2)}) collective-permute-start(bf16[256,6,64]{0,2,1:T(8,128)(2,1)S(1)} %bitcast.272), channel_id=1, source_target_pairs={{0,1},{1,2},{2,3},{3,4},{4,5},{5,6},{6,7},{7,8},{8,9},{9,10},{10,1... | collective-permute-start | bytes 589832 | tf_op jit(solution)/shard_map/ppermute | solution.py:19
  85.5 21.0 %collective-permute-start.4 = (bf16[256,6,64]{0,2,1:T(8,128)(2,1)S(1)}, bf16[256,6,64]{0,2,1:T(8,128)(2,1)}, u32[]{:S(2)}, u32[]{:S(2)}) collective-permute-start(bf16[256,6,64]{0,2,1:T(8,128)(2,1)S(1)} %bitcast.273), channel_id=1, source_target_pairs={{0,2},{1,3},{2,4},{3,5},{4,6},{5,7},{6,8},{7,9},{8,10},{9,11},{10,... | collective-permute-start | bytes 589832 | tf_op jit(solution)/shard_map/ppermute | solution.py:19
  88.9 9.7 %collective-permute-start.3 = (bf16[256,6,64]{0,2,1:T(8,128)(2,1)S(1)}, bf16[256,6,64]{0,2,1:T(8,128)(2,1)S(1)}, u32[]{:S(2)}, u32[]{:S(2)}) collective-permute-start(bf16[256,6,64]{0,2,1:T(8,128)(2,1)S(1)} %copy-done.32), channel_id=1, source_target_pairs={{0,1},{1,2},{2,3},{3,4},{4,5},{5,6},{6,7},{7,8},{8,9},{9,10},{10,1... | collective-permute-start | bytes 589832 | tf_op jit(solution)/shard_map/ppermute | solution.py:19
  90.9 13.2 %collective-permute-start.2 = (bf16[256,6,64]{0,2,1:T(8,128)(2,1)S(1)}, bf16[256,6,64]{0,2,1:T(8,128)(2,1)S(1)}, u32[]{:S(2)}, u32[]{:S(2)}) collective-permute-start(bf16[256,6,64]{0,2,1:T(8,128)(2,1)S(1)} %copy-done.32), channel_id=1, source_target_pairs={{0,2},{1,3},{2,4},{3,5},{4,6},{5,7},{6,8},{7,9},{8,10},{9,11},{10,... | collective-permute-start | bytes 589832 | tf_op jit(solution)/shard_map/ppermute | solution.py:19
  92.7 17.7 %collective-permute-start.1 = (bf16[256,6,64]{0,2,1:T(8,128)(2,1)S(1)}, bf16[256,6,64]{0,2,1:T(8,128)(2,1)S(1)}, u32[]{:S(2)}, u32[]{:S(2)}) collective-permute-start(bf16[256,6,64]{0,2,1:T(8,128)(2,1)S(1)} %bitcast.268), channel_id=1, source_target_pairs={{0,1},{1,2},{2,3},{3,4},{4,5},{5,6},{6,7},{7,8},{8,9},{9,10},{10,1... | collective-permute-start | bytes 589832 | tf_op jit(solution)/shard_map/ppermute | solution.py:19
  98.7 11.7 %collective-permute-start = (bf16[256,6,64]{0,2,1:T(8,128)(2,1)S(1)}, bf16[256,6,64]{0,2,1:T(8,128)(2,1)S(1)}, u32[]{:S(2)}, u32[]{:S(2)}) collective-permute-start(bf16[256,6,64]{0,2,1:T(8,128)(2,1)S(1)} %bitcast.269), channel_id=1, source_target_pairs={{0,2},{1,3},{2,4},{3,5},{4,6},{5,7},{6,8},{7,9},{8,10},{9,11},{10,... | collective-permute-start | bytes 589832 | tf_op jit(solution)/shard_map/ppermute | solution.py:19
  113.4 106.1 %all-gather.7.cloned.1.call-start = ((), (), s32[]{:S(2)}) async-start(), calls=%async_computation.6 | async-start | bytes 5013504 | tf_op jit(solution)/shard_map/all_gather | solution.py:210
  114.3 197.6 %reduce-scatter.16.cloned.1.call-start = ((), (), s32[]{:S(2)}) async-start(), calls=%async_computation.11 | async-start | bytes 5013504
  165.2 290.5 %copy-start.73 = (f32[256]{0:T(256)}, f32[256]{0:T(256)S(1)}, u32[]{:S(2)}) copy-start(f32[256]{0:T(256)S(1)} %add_rsqrt_fusion.2) | copy-start | bytes 3076
  165.2 290.5 %copy-start.77 = (f32[256]{0:T(256)}, f32[256]{0:T(256)S(1)}, u32[]{:S(2)}) copy-start(f32[256]{0:T(256)S(1)} %add_rsqrt_fusion) | copy-start | bytes 3076
  237.6 74.3 %copy-start.56 = (f32[48,1536]{1,0:T(8,128)S(1)}, f32[48,1536]{1,0:T(8,128)}, u32[]{:S(2)}) copy-start(f32[48,1536]{1,0:T(8,128)} %param.34) | copy-start | bytes 884740
  237.7 118.5 %all-gather.9.cloned.1.call-start = ((), (), s32[]{:S(2)}) async-start(), calls=%async_computation.7 | async-start | bytes 2506752 | tf_op jit(solution)/shard_map/all_gather | solution.py:211
  314.3 103.5 %all-reduce.13.cloned.1.call-start = ((), (), s32[]{:S(2)}) async-start(), calls=%async_computation.14 | async-start | bytes 3145728 | tf_op jit(solution)/shard_map/psum | solution.py:124
  367.4 88.3 %all-reduce.17.cloned.1.call-start = ((), (), s32[]{:S(2)}) async-start(), calls=%async_computation.16 | async-start | bytes 1572864 | tf_op jit(solution)/shard_map/psum | solution.py:111
  373.8 213.6 %all-reduce.11.cloned.1.call-start = ((), (), s32[]{:S(2)}) async-start(), calls=%async_computation.13 | async-start | bytes 3145728 | tf_op jit(solution)/shard_map/psum | solution.py:173
  468.6 30.6 %collective-permute-start.10 = (bf16[256,6,64]{0,2,1:T(8,128)(2,1)}, bf16[256,6,64]{0,2,1:T(8,128)(2,1)}, u32[]{:S(2)}, u32[]{:S(2)}) collective-permute-start(bf16[256,6,64]{0,2,1:T(8,128)(2,1)} %get-tuple-element.169), channel_id=1, source_target_pairs={{1,0},{2,1},{3,2},{4,3},{5,4},{6,5},{7,6},{8,7},{9,8},{10,9},{11,1... | collective-permute-start | bytes 589832 | tf_op jit(solution)/shard_map/ppermute | solution.py:19
  469.9 30.7 %collective-permute-start.11 = (bf16[256,6,64]{0,2,1:T(8,128)(2,1)}, bf16[256,6,64]{0,2,1:T(8,128)(2,1)}, u32[]{:S(2)}, u32[]{:S(2)}) collective-permute-start(bf16[256,6,64]{0,2,1:T(8,128)(2,1)} %get-tuple-element.170), channel_id=1, source_target_pairs={{2,0},{3,1},{4,2},{5,3},{6,4},{7,5},{8,6},{9,7},{10,8},{11,9},{12,... | collective-permute-start | bytes 589832 | tf_op jit(solution)/shard_map/ppermute | solution.py:19
  476.3 29.2 %collective-permute-start.14 = (bf16[256,6,64]{0,2,1:T(8,128)(2,1)}, bf16[256,6,64]{0,2,1:T(8,128)(2,1)}, u32[]{:S(2)}, u32[]{:S(2)}) collective-permute-start(bf16[256,6,64]{0,2,1:T(8,128)(2,1)} %get-tuple-element.173), channel_id=1, source_target_pairs={{1,0},{2,1},{3,2},{4,3},{5,4},{6,5},{7,6},{8,7},{9,8},{10,9},{11,1... | collective-permute-start | bytes 589832 | tf_op jit(solution)/shard_map/ppermute | solution.py:19
  477.6 29.2 %collective-permute-start.15 = (bf16[256,6,64]{0,2,1:T(8,128)(2,1)}, bf16[256,6,64]{0,2,1:T(8,128)(2,1)}, u32[]{:S(2)}, u32[]{:S(2)}) collective-permute-start(bf16[256,6,64]{0,2,1:T(8,128)(2,1)} %get-tuple-element.174), channel_id=1, source_target_pairs={{2,0},{3,1},{4,2},{5,3},{6,4},{7,5},{8,6},{9,7},{10,8},{11,9},{12,... | collective-permute-start | bytes 589832 | tf_op jit(solution)/shard_map/ppermute | solution.py:19
  483.9 26.5 %collective-permute-start.12 = (bf16[256,6,64]{0,2,1:T(8,128)(2,1)}, bf16[256,6,64]{0,2,1:T(8,128)(2,1)}, u32[]{:S(2)}, u32[]{:S(2)}) collective-permute-start(bf16[256,6,64]{0,2,1:T(8,128)(2,1)} %get-tuple-element.171), channel_id=1, source_target_pairs={{1,0},{2,1},{3,2},{4,3},{5,4},{6,5},{7,6},{8,7},{9,8},{10,9},{11,1... | collective-permute-start | bytes 589832 | tf_op jit(solution)/shard_map/ppermute | solution.py:19
  499.2 12.5 %collective-permute-start.13 = (bf16[256,6,64]{0,2,1:T(8,128)(2,1)}, bf16[256,6,64]{0,2,1:T(8,128)(2,1)}, u32[]{:S(2)}, u32[]{:S(2)}) collective-permute-start(bf16[256,6,64]{0,2,1:T(8,128)(2,1)} %get-tuple-element.172), channel_id=1, source_target_pairs={{2,0},{3,1},{4,2},{5,3},{6,4},{7,5},{8,6},{9,7},{10,8},{11,9},{12,... | collective-permute-start | bytes 589832 | tf_op jit(solution)/shard_map/ppermute | solution.py:19
  500.5 11.2 %collective-permute-start.8 = (bf16[256,6,64]{0,2,1:T(8,128)(2,1)}, bf16[256,6,64]{0,2,1:T(8,128)(2,1)}, u32[]{:S(2)}, u32[]{:S(2)}) collective-permute-start(bf16[256,6,64]{0,2,1:T(8,128)(2,1)} %get-tuple-element.167), channel_id=1, source_target_pairs={{1,0},{2,1},{3,2},{4,3},{5,4},{6,5},{7,6},{8,7},{9,8},{10,9},{11,1... | collective-permute-start | bytes 589832 | tf_op jit(solution)/shard_map/ppermute | solution.py:19
  505.5 13.8 %collective-permute-start.9 = (bf16[256,6,64]{0,2,1:T(8,128)(2,1)}, bf16[256,6,64]{0,2,1:T(8,128)(2,1)}, u32[]{:S(2)}, u32[]{:S(2)}) collective-permute-start(bf16[256,6,64]{0,2,1:T(8,128)(2,1)} %get-tuple-element.168), channel_id=1, source_target_pairs={{2,0},{3,1},{4,2},{5,3},{6,4},{7,5},{8,6},{9,7},{10,8},{11,9},{12,... | collective-permute-start | bytes 589832 | tf_op jit(solution)/shard_map/ppermute | solution.py:19
  531.8 118.0 %reduce-scatter.12.cloned.1.call-start = ((), (), s32[]{:S(2)}) async-start(), calls=%async_computation.9 | async-start | bytes 1253376 | tf_op jit(solution)/shard_map/reduce_scatter | solution.py:219
  534.8 173.9 %reduce-scatter.18.cloned.1.call-start = ((), (), s32[]{:S(2)}) async-start(), calls=%async_computation.12 | async-start | bytes 417792
  536.7 50.6 %copy-start.82 = (f32[256]{0:T(256)S(1)}, f32[256]{0:T(256)}, u32[]{:S(2)}) copy-start(f32[256]{0:T(256)} %copy-done.81) | copy-start | bytes 3076
  540.3 51.9 %copy-start.48 = (bf16[256,1,384]{2,0,1:T(8,128)(2,1)S(1)}, bf16[256,1,384]{2,0,1:T(8,128)(2,1)}, u32[]{:S(2)}) copy-start(bf16[256,1,384]{2,0,1:T(8,128)(2,1)} %copy.164) | copy-start | bytes 589828
  540.3 51.9 %copy-start.49 = (bf16[256,1,384]{2,0,1:T(8,128)(2,1)S(1)}, bf16[256,1,384]{2,0,1:T(8,128)(2,1)}, u32[]{:S(2)}) copy-start(bf16[256,1,384]{2,0,1:T(8,128)(2,1)} %copy.166) | copy-start | bytes 589828
  592.1 188.2 %reduce-scatter.10.cloned.1.call-start = ((), (), s32[]{:S(2)}) async-start(), calls=%async_computation.8 | async-start | bytes 3760128 | tf_op jit(solution)/shard_map/reduce_scatter | solution.py:218
  597.0 297.3 %reduce-scatter.14.cloned.1.call-start = ((), (), s32[]{:S(2)}) async-start(), calls=%async_computation.10 | async-start | bytes 10027008 | tf_op jit(solution)/shard_map/reduce_scatter | solution.py:220
  611.2 38.6 %copy-start.57 = (f32[48,384]{1,0:T(8,128)S(1)}, f32[48,384]{1,0:T(8,128)}, u32[]{:S(2)}) copy-start(f32[48,384]{1,0:T(8,128)} %param.22) | copy-start | bytes 221188
  611.2 98.3 %copy-start.88 = (f32[48,2]{0,1:T(2,128)S(1)}, f32[48,2]{0,1:T(2,128)}, u32[]{:S(2)}) copy-start(f32[48,2]{0,1:T(2,128)} %param.25) | copy-start | bytes 1156
  611.2 98.3 %copy-start.89 = (f32[48,2]{0,1:T(2,128)S(1)}, f32[48,2]{0,1:T(2,128)}, u32[]{:S(2)}) copy-start(f32[48,2]{0,1:T(2,128)} %param.35) | copy-start | bytes 1156
  611.3 98.2 %copy-start.90 = (f32[48,2]{0,1:T(2,128)S(1)}, f32[48,2]{0,1:T(2,128)}, u32[]{:S(2)}) copy-start(f32[48,2]{0,1:T(2,128)} %param.30) | copy-start | bytes 1156
  611.3 169.1 %copy-start.25 = (f32[48,3,384]{2,0,1:T(8,128)S(1)}, f32[48,3,384]{2,0,1:T(8,128)}, u32[]{:S(2)}) copy-start(f32[48,3,384]{2,0,1:T(8,128)} %param.21) | copy-start | bytes 663556
  611.3 169.1 %copy-start.60 = (f32[48,3,384]{2,0,1:T(8,128)S(1)}, f32[48,3,384]{2,0,1:T(8,128)}, u32[]{:S(2)}) copy-start(f32[48,3,384]{2,0,1:T(8,128)} %param.31) | copy-start | bytes 663556
  611.3 169.1 %copy-start.61 = (f32[48,3,384]{2,0,1:T(8,128)S(1)}, f32[48,3,384]{2,0,1:T(8,128)}, u32[]{:S(2)}) copy-start(f32[48,3,384]{2,0,1:T(8,128)} %param.26) | copy-start | bytes 663556
  612.6 281.7 %copy-start.18 = (f32[48,2,1536]{2,1,0:T(2,128)S(1)}, f32[48,2,1536]{2,1,0:T(2,128)}, u32[]{:S(2)}) copy-start(f32[48,2,1536]{2,1,0:T(2,128)} %param.23) | copy-start | bytes 1769476
  612.6 281.7 %copy-start.54 = (f32[48,2,1536]{2,1,0:T(2,128)S(1)}, f32[48,2,1536]{2,1,0:T(2,128)}, u32[]{:S(2)}) copy-start(f32[48,2,1536]{2,1,0:T(2,128)} %param.33) | copy-start | bytes 1769476
  612.6 281.7 %copy-start.55 = (f32[48,2,1536]{2,1,0:T(2,128)S(1)}, f32[48,2,1536]{2,1,0:T(2,128)}, u32[]{:S(2)}) copy-start(f32[48,2,1536]{2,1,0:T(2,128)} %param.28) | copy-start | bytes 1769476
  709.5 186.3 %copy-start.87 = (f32[48,2]{0,1:T(2,128)}, f32[48,2]{0,1:T(2,128)S(1)}, u32[]{:S(2)}) copy-start(f32[48,2]{0,1:T(2,128)S(1)} %copy.192) | copy-start | bytes 1156
  (81 other events, 458.3 us)
Sparse Core Ops, SparseCore 0:
  10.9 45.0 all-gather.4
  113.6 49.9 all-reduce.14
  166.4 53.1 all-gather.6
  237.8 74.1 reduce-scatter.15
  314.7 41.4 all-gather.8
  367.5 50.2 all-reduce.12
  421.3 34.3 all-reduce.16
  531.9 55.4 all-reduce.10
  591.5 58.1 reduce-scatter.11
  653.7 54.9 reduce-scatter.17
  713.1 67.1 reduce-scatter.9
  784.3 109.9 reduce-scatter.13
where the time goes:
time: 916 us; the launch traced here: 908 us
  waiting for transfers between devices  632 us (69%)
  matrix products  85 us (9%)
  other arithmetic  49.9 us (5%)
  local copies, waits for them, and re-layouts  48.6 us (5%)
  blocking collectives  44.1 us (5%)
  starting transfers between devices  32.5 us (4%)
  between operations  16 us (2%)
    unnamed x14, waiting for transfers between devices  132 us
    reduce_scatter x1, waiting for transfers between devices, body(): lax.psum_scatter(local_grads[2], 'dp', scatter_dimension=0, tiled=True)  112 us
    reduce_scatter x1, waiting for transfers between devices, body(): lax.psum_scatter(local_grads[0], 'dp', scatter_dimension=0, tiled=True)  70.2 us
    all_gather x1, waiting for transfers between devices, body(): lax.all_gather(shards[2], 'dp', axis=0, tiled=True)  54.3 us
    psum x1, waiting for transfers between devices, micro_step(): branch = lax.psum(branch, 'tensor')  49.1 us
    psum x1, waiting for transfers between devices, micro_step(): grad_normed_one = lax.psum(grad_normed_one, 'tensor')  47 us
    psum x1, waiting for transfers between devices, micro_step(): grad_normed_two = lax.psum(grad_normed_two, 'tensor')  44 us
    all_gather x1, waiting for transfers between devices, body(): lax.all_gather(shards[3], 'dp', axis=0, tiled=True)  41.7 us
  transfers between devices with their start and end apart: 28, of which 13 were waited for; matrix products, arithmetic and copies ran while one was open for 11% of the time, Pallas kernels for 0%

commit v1 on v0

--- a/solution.py
+++ b/solution.py
@@ -58,6 +58,10 @@
 
 
 def micro_step(tokens, upstream, seg_row, whole, rank):
+
+    def number_turns(load):
+        return jnp.sum(jax.lax.all_gather(load, axis_name="tensor"), axis=0)
+
     qkv_full, out_full, gateup_full, down_full, gains_full = whole
     gain_one = gains_full[:, 0].astype(jnp.float32)
     gain_two = gains_full[:, 1].astype(jnp.float32)
@@ -108,7 +112,7 @@
     active = gate * sigma
     hidden = (active * upward).astype(jnp.bfloat16)
     down_part = jnp.einsum("tf,df->td", hidden, down_full, preferred_element_type=jnp.float32)
-    down_part = lax.psum(down_part.astype(jnp.bfloat16), "tensor").astype(jnp.float32)
+    down_part = number_turns(down_part.astype(jnp.bfloat16)).astype(jnp.float32)
     result = (resid + down_part).astype(jnp.bfloat16)
     grad_hidden = jnp.einsum("td,df->tf", upstream, down_full, preferred_element_type=jnp.float32)
     down_grad = jnp.einsum("td,tf->df", upstream, hidden, preferred_element_type=jnp.float32)

time: 916 us -> 887 us (0.968)
  waiting for transfers between devices: 632 us -> 569 us
  blocking collectives: 44.1 us -> 76.2 us
    psum x1 -> x0, waiting for transfers between devices: 35.5 us -> none  [micro_step(): lax.psum(down_part.astype(jnp.bfloat16), 'tensor').astype(jnp.float32)]
    all_gather x0 -> x2, blocking collectives: none -> 32 us  [number_turns(): return jnp.sum(jax.lax.all_gather(load, axis_name='tensor'), axis=0)]
    psum x1, waiting for transfers between devices: 44 us -> 16.3 us  [micro_step(): grad_normed_two = lax.psum(grad_normed_two, 'tensor')]
    unnamed x14 -> x13, waiting for transfers between devices: 132 us -> 132 us
    unnamed x211 -> x215, local copies, waits for them, and re-layouts: 21.6 us -> 21.7 us
  transfers between devices with their start and end apart: 28 -> 27, of which waited for: 13 -> 12; matrix products, arithmetic and copies ran while one was open for 11% -> 11% of each run, Pallas kernels for 0% -> 0%
where the time goes in v1:
time: 887 us; the launch traced here: 880 us
  waiting for transfers between devices  569 us (64%)
  matrix products  85.9 us (10%)
  blocking collectives  76.2 us (9%)
  other arithmetic  51.7 us (6%)
  local copies, waits for them, and re-layouts  48.7 us (5%)
  starting transfers between devices  32.5 us (4%)
  between operations  15.7 us (2%)
    unnamed x13, waiting for transfers between devices  132 us
    reduce_scatter x1, waiting for transfers between devices, body(): lax.psum_scatter(local_grads[2], 'dp', scatter_dimension=0, tiled=True)  112 us
    reduce_scatter x1, waiting for transfers between devices, body(): lax.psum_scatter(local_grads[0], 'dp', scatter_dimension=0, tiled=True)  70 us
    all_gather x1, waiting for transfers between devices, body(): lax.all_gather(shards[2], 'dp', axis=0, tiled=True)  54.3 us
    psum x1, waiting for transfers between devices, micro_step(): branch = lax.psum(branch, 'tensor')  49.2 us
    psum x1, waiting for transfers between devices, micro_step(): grad_normed_one = lax.psum(grad_normed_one, 'tensor')  47 us
    all_gather x1, waiting for transfers between devices, body(): lax.all_gather(shards[3], 'dp', axis=0, tiled=True)  41.7 us
    reduce_scatter x1, waiting for transfers between devices, body(): lax.psum_scatter(local_grads[1], 'dp', scatter_dimension=0, tiled=True)  37.2 us
  transfers between devices with their start and end apart: 27, of which 12 were waited for; matrix products, arithmetic and copies ran while one was open for 11% of the time, Pallas kernels for 0%

profile of v1, /device:TPU:0, one launch (start us, length us, event | category | flops | bytes accessed | tf_op | source)
XLA Modules:
  0.0 879.7 jit_solution(1725547502948946318)
XLA Ops:
  9.7 23.1 %all-gather.2 = bf16[16,48,2]{1,2,0:T(2,128)(2,1)S(1)} all-gather(bf16[1,48,2]{1,2,0:T(2,128)(2,1)S(1)} %convert_bitcast_fusion), channel_id=1, replica_groups=mesh['tensor'=2,'dp'=16] {'dp'}, dimensions={0}, use_global_device_ids=true | all-gather | bytes 3264 | tf_op jit(solution)/shard_map/all_gather | solution.py:216
  37.1 21.0 %all_gather.34 = bf16[768,384]{1,0:T(8,128)(2,1)S(1)} all-gather(bf16[48,384]{1,0:T(8,128)(2,1)S(1)} %convert_element_type.232), channel_id=1, replica_groups=mesh['tensor'=2,'dp'=16] {'dp'}, dimensions={0}, use_global_device_ids=true | all-gather | bytes 626688 | tf_op jit(solution)/shard_map/all_gather | solution.py:213
  58.1 2.2 fusion.152
  64.1 2.2 fusion.149
  74.3 2.4 fusion.91
  76.7 3.1 collective-permute-start.7
  79.8 2.8 collective-permute-start.6
  85.5 2.2 collective-permute-start.4
  92.7 2.3 collective-permute-start.1
  95.0 2.3 fusion.161
  98.7 5.4 collective-permute-start
  106.6 2.5 fusion.44
  114.4 49.2 %all-reduce.13.cloned.1.call-done = (f32[256,768]{1,0:T(8,128)}, f32[256,768]{1,0:T(8,128)}) async-done(((f32[256,768]{1,0:T(8,128)}, f32[256,768]{1,0:T(8,128)}), (f32[256,768]{1,0:T(8,128)}, f32[256,768]{1,0:T(8,128)})) %all-reduce.13.cloned.1.call-update) | async-done | bytes 1572880 | tf_op jit(solution)/shard_map/psum | solution.py:105
  165.2 54.3 %all-gather.9.cloned.1.call-done = bf16[768,2,1536]{2,0,1:T(8,128)(2,1)} async-done(((bf16[48,2,1536]{2,0,1:T(8,128)(2,1)}), bf16[768,2,1536]{2,0,1:T(8,128)(2,1)}) %all-gather.9.cloned.1.call-update) | async-done | bytes 4718608 | tf_op jit(solution)/shard_map/all_gather | solution.py:214
  219.6 3.9 fusion.124
  228.3 3.3 add_bitcast_fusion
  231.6 6.1 copy.189
  237.8 74.3 %reduce-scatter.16.cloned.1.call-done = f32[48,1536]{1,0:T(8,128)} async-done(((f32[768,1536]{1,0:T(8,128)}), f32[48,1536]{1,0:T(8,128)}) %reduce-scatter.16.cloned.1.call-update) | async-done | bytes 294928
  312.1 2.3 multiply_add_fusion.2
  314.6 41.7 %all-gather.11.cloned.1.call-done = bf16[768,1536]{1,0:T(8,128)(2,1)} async-done(((bf16[48,1536]{1,0:T(8,128)(2,1)}), bf16[768,1536]{1,0:T(8,128)(2,1)}) %all-gather.11.cloned.1.call-update) | async-done | bytes 2359312 | tf_op jit(solution)/shard_map/all_gather | solution.py:215
  356.3 3.9 fusion.73
  362.8 2.3 convolution_bitcast_fusion.1
  365.1 2.3 convolution_bitcast_fusion
  367.5 3.6 convolution_convert_fusion
  371.2 20.9 %all-gather.1 = bf16[512,768]{1,0:T(8,128)(2,1)} all-gather(bf16[256,768]{1,0:T(8,128)(2,1)S(1)} %convolution_convert_fusion), channel_id=3, replica_groups=mesh['tensor'=2,'dp'=16] {'tensor'}, dimensions={0}, use_global_device_ids=true | all-gather | bytes 1179648 | tf_op jit(solution)/shard_map/all_gather | solution.py:63
  393.3 3.6 convolution_convert_fusion.1
  397.0 11.2 %all-gather = bf16[512,768]{1,0:T(8,128)(2,1)} all-gather(bf16[256,768]{1,0:T(8,128)(2,1)S(1)} %convolution_convert_fusion.1), channel_id=2, replica_groups=mesh['tensor'=2,'dp'=16] {'tensor'}, dimensions={0}, use_global_device_ids=true | all-gather | bytes 1179648 | tf_op jit(solution)/shard_map/all_gather | solution.py:63
  408.1 2.2 reduce_sum.171
  410.3 16.3 %all-reduce.11.cloned.1.call-done = (f32[256,768]{1,0:T(8,128)}, f32[256,768]{1,0:T(8,128)}) async-done(((f32[256,768]{1,0:T(8,128)}, f32[256,768]{1,0:T(8,128)}), (f32[256,768]{1,0:T(8,128)}, f32[256,768]{1,0:T(8,128)})) %all-reduce.11.cloned.1.call-update) | async-done | bytes 1572880 | tf_op jit(solution)/shard_map/psum | solution.py:128
  426.6 2.6 multiply_reduce_fusion.3
  435.1 4.4 fusion.166
  442.9 4.3 fusion.163
  450.9 2.4 multiply_reduce_fusion
  461.8 2.0 convolution_bitcast_fusion.4
  483.5 7.5 collective-permute-done.9
  492.5 2.3 fusion.97
  498.4 3.4 convolution_bitcast_fusion.2
  508.4 3.6 fusion.110
  512.0 47.0 %all-reduce.9.cloned.1.call-done = (f32[256,768]{1,0:T(8,128)}, f32[256,768]{1,0:T(8,128)}) async-done(((f32[256,768]{1,0:T(8,128)}, f32[256,768]{1,0:T(8,128)}), (f32[256,768]{1,0:T(8,128)}, f32[256,768]{1,0:T(8,128)})) %all-reduce.9.cloned.1.call-update) | async-done | bytes 1572880 | tf_op jit(solution)/shard_map/psum | solution.py:177
  559.1 2.5 fusion.53
  563.9 4.8 convolution_add_fusion.1
  569.4 3.0 fusion.46
  572.4 5.2 convolution_add_fusion
  578.7 2.0 pad_maximum_fusion.7
  584.3 37.2 %reduce-scatter.12.cloned.1.call-done = f32[48,384]{1,0:T(8,128)} async-done(((f32[768,384]{1,0:T(8,128)}), f32[48,384]{1,0:T(8,128)}) %reduce-scatter.12.cloned.1.call-update) | async-done | bytes 73744 | tf_op jit(solution)/shard_map/reduce_scatter | solution.py:223
  623.1 57.6 %reduce-scatter.18.cloned.1.call-done = f32[48,2]{1,0:T(8,128)} async-done(((f32[768,2]{1,0:T(8,128)}), f32[48,2]{1,0:T(8,128)}) %reduce-scatter.18.cloned.1.call-update) | async-done | bytes 400
  682.0 70.0 %reduce-scatter.10.cloned.1.call-done = f32[48,3,384]{2,0,1:T(8,128)} async-done(((f32[768,3,384]{2,0,1:T(8,128)}), f32[48,3,384]{2,0,1:T(8,128)}) %reduce-scatter.10.cloned.1.call-update) | async-done | bytes 221200 | tf_op jit(solution)/shard_map/reduce_scatter | solution.py:222
  753.9 112.3 %reduce-scatter.14.cloned.1.call-done = f32[48,2,1536]{2,0,1:T(8,128)} async-done(((f32[768,2,1536]{2,0,1:T(8,128)}), f32[48,2,1536]{2,0,1:T(8,128)}) %reduce-scatter.14.cloned.1.call-update) | async-done | bytes 589840 | tf_op jit(solution)/shard_map/reduce_scatter | solution.py:224
  (359 shorter events, 117.0 us)
Async XLA Ops:
  7.2 50.9 %copy-start.2 = (bf16[2,256,768]{2,1,0:T(8,128)(2,1)S(1)}, bf16[2,256,768]{2,1,0:T(8,128)(2,1)}, u32[]{:S(2)}) copy-start(bf16[2,256,768]{2,1,0:T(8,128)(2,1)} %param.18) | copy-start | bytes 2359300
  7.2 50.9 %all-gather.7.cloned.1.call-start = ((), (), s32[]{:S(2)}) async-start(), calls=%async_computation.5 | async-start | bytes 1880064 | tf_op jit(solution)/shard_map/all_gather | solution.py:212
  8.9 154.6 %all-reduce.13.cloned.1.call-start = ((), (), s32[]{:S(2)}) async-start(), calls=%async_computation.15 | async-start | bytes 3145728 | tf_op jit(solution)/shard_map/psum | solution.py:105
  35.6 38.6 %copy-start.54 = (f32[256,64]{0,1:T(8,128)}, f32[256,64]{0,1:T(8,128)S(1)}, u32[]{:S(2)}) copy-start(f32[256,64]{0,1:T(8,128)S(1)} %get-tuple-element.205) | copy-start | bytes 196612
  35.6 38.6 %copy-start.56 = (f32[256,64]{0,1:T(8,128)}, f32[256,64]{0,1:T(8,128)S(1)}, u32[]{:S(2)}) copy-start(f32[256,64]{0,1:T(8,128)S(1)} %get-tuple-element.204) | copy-start | bytes 196612
  76.7 14.2 %collective-permute-start.7 = (bf16[256,6,64]{0,2,1:T(8,128)(2,1)}, bf16[256,6,64]{0,2,1:T(8,128)(2,1)}, u32[]{:S(2)}, u32[]{:S(2)}) collective-permute-start(bf16[256,6,64]{0,2,1:T(8,128)(2,1)} %get-tuple-element.192), channel_id=1, source_target_pairs={{0,1},{1,2},{2,3},{3,4},{4,5},{5,6},{6,7},{7,8},{8,9},{9,10},{10,1... | collective-permute-start | bytes 589832 | tf_op jit(solution)/shard_map/ppermute | solution.py:19
  79.8 12.9 %collective-permute-start.6 = (bf16[256,6,64]{0,2,1:T(8,128)(2,1)}, bf16[256,6,64]{0,2,1:T(8,128)(2,1)}, u32[]{:S(2)}, u32[]{:S(2)}) collective-permute-start(bf16[256,6,64]{0,2,1:T(8,128)(2,1)} %get-tuple-element.192), channel_id=1, source_target_pairs={{0,2},{1,3},{2,4},{3,5},{4,6},{5,7},{6,8},{7,9},{8,10},{9,11},{10,... | collective-permute-start | bytes 589832 | tf_op jit(solution)/shard_map/ppermute | solution.py:19
  83.9 22.6 %collective-permute-start.5 = (bf16[256,6,64]{0,2,1:T(8,128)(2,1)S(1)}, bf16[256,6,64]{0,2,1:T(8,128)(2,1)S(1)}, u32[]{:S(2)}, u32[]{:S(2)}) collective-permute-start(bf16[256,6,64]{0,2,1:T(8,128)(2,1)S(1)} %bitcast.276), channel_id=1, source_target_pairs={{0,1},{1,2},{2,3},{3,4},{4,5},{5,6},{6,7},{7,8},{8,9},{9,10},{10,1... | collective-permute-start | bytes 589832 | tf_op jit(solution)/shard_map/ppermute | solution.py:19
  85.5 21.0 %collective-permute-start.4 = (bf16[256,6,64]{0,2,1:T(8,128)(2,1)S(1)}, bf16[256,6,64]{0,2,1:T(8,128)(2,1)}, u32[]{:S(2)}, u32[]{:S(2)}) collective-permute-start(bf16[256,6,64]{0,2,1:T(8,128)(2,1)S(1)} %bitcast.277), channel_id=1, source_target_pairs={{0,2},{1,3},{2,4},{3,5},{4,6},{5,7},{6,8},{7,9},{8,10},{9,11},{10,... | collective-permute-start | bytes 589832 | tf_op jit(solution)/shard_map/ppermute | solution.py:19
  89.0 9.7 %collective-permute-start.3 = (bf16[256,6,64]{0,2,1:T(8,128)(2,1)S(1)}, bf16[256,6,64]{0,2,1:T(8,128)(2,1)S(1)}, u32[]{:S(2)}, u32[]{:S(2)}) collective-permute-start(bf16[256,6,64]{0,2,1:T(8,128)(2,1)S(1)} %copy-done.35), channel_id=1, source_target_pairs={{0,1},{1,2},{2,3},{3,4},{4,5},{5,6},{6,7},{7,8},{8,9},{9,10},{10,1... | collective-permute-start | bytes 589832 | tf_op jit(solution)/shard_map/ppermute | solution.py:19
  90.9 13.1 %collective-permute-start.2 = (bf16[256,6,64]{0,2,1:T(8,128)(2,1)S(1)}, bf16[256,6,64]{0,2,1:T(8,128)(2,1)S(1)}, u32[]{:S(2)}, u32[]{:S(2)}) collective-permute-start(bf16[256,6,64]{0,2,1:T(8,128)(2,1)S(1)} %copy-done.35), channel_id=1, source_target_pairs={{0,2},{1,3},{2,4},{3,5},{4,6},{5,7},{6,8},{7,9},{8,10},{9,11},{10,... | collective-permute-start | bytes 589832 | tf_op jit(solution)/shard_map/ppermute | solution.py:19
  92.7 17.7 %collective-permute-start.1 = (bf16[256,6,64]{0,2,1:T(8,128)(2,1)S(1)}, bf16[256,6,64]{0,2,1:T(8,128)(2,1)S(1)}, u32[]{:S(2)}, u32[]{:S(2)}) collective-permute-start(bf16[256,6,64]{0,2,1:T(8,128)(2,1)S(1)} %bitcast.272), channel_id=1, source_target_pairs={{0,1},{1,2},{2,3},{3,4},{4,5},{5,6},{6,7},{7,8},{8,9},{9,10},{10,1... | collective-permute-start | bytes 589832 | tf_op jit(solution)/shard_map/ppermute | solution.py:19
  98.7 11.7 %collective-permute-start = (bf16[256,6,64]{0,2,1:T(8,128)(2,1)S(1)}, bf16[256,6,64]{0,2,1:T(8,128)(2,1)S(1)}, u32[]{:S(2)}, u32[]{:S(2)}) collective-permute-start(bf16[256,6,64]{0,2,1:T(8,128)(2,1)S(1)} %bitcast.273), channel_id=1, source_target_pairs={{0,2},{1,3},{2,4},{3,5},{4,6},{5,7},{6,8},{7,9},{8,10},{9,11},{10,... | collective-permute-start | bytes 589832 | tf_op jit(solution)/shard_map/ppermute | solution.py:19
  113.4 106.1 %all-gather.9.cloned.1.call-start = ((), (), s32[]{:S(2)}) async-start(), calls=%async_computation.6 | async-start | bytes 5013504 | tf_op jit(solution)/shard_map/all_gather | solution.py:214
  114.3 197.7 %reduce-scatter.16.cloned.1.call-start = ((), (), s32[]{:S(2)}) async-start(), calls=%async_computation.11 | async-start | bytes 5013504
  165.2 264.0 %copy-start.76 = (f32[256]{0:T(256)}, f32[256]{0:T(256)S(1)}, u32[]{:S(2)}) copy-start(f32[256]{0:T(256)S(1)} %add_rsqrt_fusion.2) | copy-start | bytes 3076
  165.2 264.0 %copy-start.80 = (f32[256]{0:T(256)}, f32[256]{0:T(256)S(1)}, u32[]{:S(2)}) copy-start(f32[256]{0:T(256)S(1)} %add_rsqrt_fusion) | copy-start | bytes 3076
  237.7 74.3 %copy-start.59 = (f32[48,1536]{1,0:T(8,128)S(1)}, f32[48,1536]{1,0:T(8,128)}, u32[]{:S(2)}) copy-start(f32[48,1536]{1,0:T(8,128)} %param.34) | copy-start | bytes 884740
  237.8 118.5 %all-gather.11.cloned.1.call-start = ((), (), s32[]{:S(2)}) async-start(), calls=%async_computation.7 | async-start | bytes 2506752 | tf_op jit(solution)/shard_map/all_gather | solution.py:215
  314.3 112.2 %all-reduce.11.cloned.1.call-start = ((), (), s32[]{:S(2)}) async-start(), calls=%async_computation.14 | async-start | bytes 3145728 | tf_op jit(solution)/shard_map/psum | solution.py:128
  367.5 191.6 %all-reduce.9.cloned.1.call-start = ((), (), s32[]{:S(2)}) async-start(), calls=%async_computation.13 | async-start | bytes 3145728 | tf_op jit(solution)/shard_map/psum | solution.py:177
  440.3 30.7 %collective-permute-start.10 = (bf16[256,6,64]{0,2,1:T(8,128)(2,1)}, bf16[256,6,64]{0,2,1:T(8,128)(2,1)}, u32[]{:S(2)}, u32[]{:S(2)}) collective-permute-start(bf16[256,6,64]{0,2,1:T(8,128)(2,1)} %get-tuple-element.167), channel_id=1, source_target_pairs={{1,0},{2,1},{3,2},{4,3},{5,4},{6,5},{7,6},{8,7},{9,8},{10,9},{11,1... | collective-permute-start | bytes 589832 | tf_op jit(solution)/shard_map/ppermute | solution.py:19
  441.6 30.7 %collective-permute-start.11 = (bf16[256,6,64]{0,2,1:T(8,128)(2,1)}, bf16[256,6,64]{0,2,1:T(8,128)(2,1)}, u32[]{:S(2)}, u32[]{:S(2)}) collective-permute-start(bf16[256,6,64]{0,2,1:T(8,128)(2,1)} %get-tuple-element.168), channel_id=1, source_target_pairs={{2,0},{3,1},{4,2},{5,3},{6,4},{7,5},{8,6},{9,7},{10,8},{11,9},{12,... | collective-permute-start | bytes 589832 | tf_op jit(solution)/shard_map/ppermute | solution.py:19
  448.0 29.2 %collective-permute-start.14 = (bf16[256,6,64]{0,2,1:T(8,128)(2,1)}, bf16[256,6,64]{0,2,1:T(8,128)(2,1)}, u32[]{:S(2)}, u32[]{:S(2)}) collective-permute-start(bf16[256,6,64]{0,2,1:T(8,128)(2,1)} %get-tuple-element.171), channel_id=1, source_target_pairs={{1,0},{2,1},{3,2},{4,3},{5,4},{6,5},{7,6},{8,7},{9,8},{10,9},{11,1... | collective-permute-start | bytes 589832 | tf_op jit(solution)/shard_map/ppermute | solution.py:19
  449.3 29.2 %collective-permute-start.15 = (bf16[256,6,64]{0,2,1:T(8,128)(2,1)}, bf16[256,6,64]{0,2,1:T(8,128)(2,1)}, u32[]{:S(2)}, u32[]{:S(2)}) collective-permute-start(bf16[256,6,64]{0,2,1:T(8,128)(2,1)} %get-tuple-element.172), channel_id=1, source_target_pairs={{2,0},{3,1},{4,2},{5,3},{6,4},{7,5},{8,6},{9,7},{10,8},{11,9},{12,... | collective-permute-start | bytes 589832 | tf_op jit(solution)/shard_map/ppermute | solution.py:19
  455.8 26.3 %collective-permute-start.12 = (bf16[256,6,64]{0,2,1:T(8,128)(2,1)}, bf16[256,6,64]{0,2,1:T(8,128)(2,1)}, u32[]{:S(2)}, u32[]{:S(2)}) collective-permute-start(bf16[256,6,64]{0,2,1:T(8,128)(2,1)} %get-tuple-element.169), channel_id=1, source_target_pairs={{1,0},{2,1},{3,2},{4,3},{5,4},{6,5},{7,6},{8,7},{9,8},{10,9},{11,1... | collective-permute-start | bytes 589832 | tf_op jit(solution)/shard_map/ppermute | solution.py:19
  471.0 12.5 %collective-permute-start.13 = (bf16[256,6,64]{0,2,1:T(8,128)(2,1)}, bf16[256,6,64]{0,2,1:T(8,128)(2,1)}, u32[]{:S(2)}, u32[]{:S(2)}) collective-permute-start(bf16[256,6,64]{0,2,1:T(8,128)(2,1)} %get-tuple-element.170), channel_id=1, source_target_pairs={{2,0},{3,1},{4,2},{5,3},{6,4},{7,5},{8,6},{9,7},{10,8},{11,9},{12,... | collective-permute-start | bytes 589832 | tf_op jit(solution)/shard_map/ppermute | solution.py:19
  472.3 11.2 %collective-permute-start.8 = (bf16[256,6,64]{0,2,1:T(8,128)(2,1)}, bf16[256,6,64]{0,2,1:T(8,128)(2,1)}, u32[]{:S(2)}, u32[]{:S(2)}) collective-permute-start(bf16[256,6,64]{0,2,1:T(8,128)(2,1)} %get-tuple-element.165), channel_id=1, source_target_pairs={{1,0},{2,1},{3,2},{4,3},{5,4},{6,5},{7,6},{8,7},{9,8},{10,9},{11,1... | collective-permute-start | bytes 589832 | tf_op jit(solution)/shard_map/ppermute | solution.py:19
  477.2 13.8 %collective-permute-start.9 = (bf16[256,6,64]{0,2,1:T(8,128)(2,1)}, bf16[256,6,64]{0,2,1:T(8,128)(2,1)}, u32[]{:S(2)}, u32[]{:S(2)}) collective-permute-start(bf16[256,6,64]{0,2,1:T(8,128)(2,1)} %get-tuple-element.166), channel_id=1, source_target_pairs={{2,0},{3,1},{4,2},{5,3},{6,4},{7,5},{8,6},{9,7},{10,8},{11,9},{12,... | collective-permute-start | bytes 589832 | tf_op jit(solution)/shard_map/ppermute | solution.py:19
  503.5 118.0 %reduce-scatter.12.cloned.1.call-start = ((), (), s32[]{:S(2)}) async-start(), calls=%async_computation.9 | async-start | bytes 1253376 | tf_op jit(solution)/shard_map/reduce_scatter | solution.py:223
  506.5 174.1 %reduce-scatter.18.cloned.1.call-start = ((), (), s32[]{:S(2)}) async-start(), calls=%async_computation.12 | async-start | bytes 417792
  508.4 50.6 %copy-start.85 = (f32[256]{0:T(256)S(1)}, f32[256]{0:T(256)}, u32[]{:S(2)}) copy-start(f32[256]{0:T(256)} %copy-done.84) | copy-start | bytes 3076
  512.0 51.9 %copy-start.51 = (bf16[256,1,384]{2,0,1:T(8,128)(2,1)S(1)}, bf16[256,1,384]{2,0,1:T(8,128)(2,1)}, u32[]{:S(2)}) copy-start(bf16[256,1,384]{2,0,1:T(8,128)(2,1)} %copy.164) | copy-start | bytes 589828
  512.0 51.9 %copy-start.52 = (bf16[256,1,384]{2,0,1:T(8,128)(2,1)S(1)}, bf16[256,1,384]{2,0,1:T(8,128)(2,1)}, u32[]{:S(2)}) copy-start(bf16[256,1,384]{2,0,1:T(8,128)(2,1)} %copy.166) | copy-start | bytes 589828
  563.8 188.2 %reduce-scatter.10.cloned.1.call-start = ((), (), s32[]{:S(2)}) async-start(), calls=%async_computation.8 | async-start | bytes 3760128 | tf_op jit(solution)/shard_map/reduce_scatter | solution.py:222
  568.7 297.5 %reduce-scatter.14.cloned.1.call-start = ((), (), s32[]{:S(2)}) async-start(), calls=%async_computation.10 | async-start | bytes 10027008 | tf_op jit(solution)/shard_map/reduce_scatter | solution.py:224
  582.9 38.6 %copy-start.60 = (f32[48,384]{1,0:T(8,128)S(1)}, f32[48,384]{1,0:T(8,128)}, u32[]{:S(2)}) copy-start(f32[48,384]{1,0:T(8,128)} %param.22) | copy-start | bytes 221188
  582.9 38.6 %copy-start.78 = (f32[48,384]{1,0:T(8,128)S(1)}, f32[48,384]{1,0:T(8,128)}, u32[]{:S(2)}) copy-start(f32[48,384]{1,0:T(8,128)} %param.32) | copy-start | bytes 221188
  582.9 98.5 %copy-start.91 = (f32[48,2]{0,1:T(2,128)S(1)}, f32[48,2]{0,1:T(2,128)}, u32[]{:S(2)}) copy-start(f32[48,2]{0,1:T(2,128)} %param.25) | copy-start | bytes 1156
  582.9 98.5 %copy-start.92 = (f32[48,2]{0,1:T(2,128)S(1)}, f32[48,2]{0,1:T(2,128)}, u32[]{:S(2)}) copy-start(f32[48,2]{0,1:T(2,128)} %param.35) | copy-start | bytes 1156
  583.0 98.5 %copy-start.93 = (f32[48,2]{0,1:T(2,128)S(1)}, f32[48,2]{0,1:T(2,128)}, u32[]{:S(2)}) copy-start(f32[48,2]{0,1:T(2,128)} %param.30) | copy-start | bytes 1156
  583.0 169.1 %copy-start.28 = (f32[48,3,384]{2,0,1:T(8,128)S(1)}, f32[48,3,384]{2,0,1:T(8,128)}, u32[]{:S(2)}) copy-start(f32[48,3,384]{2,0,1:T(8,128)} %param.21) | copy-start | bytes 663556
  583.0 169.1 %copy-start.63 = (f32[48,3,384]{2,0,1:T(8,128)S(1)}, f32[48,3,384]{2,0,1:T(8,128)}, u32[]{:S(2)}) copy-start(f32[48,3,384]{2,0,1:T(8,128)} %param.31) | copy-start | bytes 663556
  583.0 169.1 %copy-start.64 = (f32[48,3,384]{2,0,1:T(8,128)S(1)}, f32[48,3,384]{2,0,1:T(8,128)}, u32[]{:S(2)}) copy-start(f32[48,3,384]{2,0,1:T(8,128)} %param.26) | copy-start | bytes 663556
  584.2 282.0 %copy-start.19 = (f32[48,2,1536]{2,1,0:T(2,128)S(1)}, f32[48,2,1536]{2,1,0:T(2,128)}, u32[]{:S(2)}) copy-start(f32[48,2,1536]{2,1,0:T(2,128)} %param.23) | copy-start | bytes 1769476
  584.3 282.0 %copy-start.57 = (f32[48,2,1536]{2,1,0:T(2,128)S(1)}, f32[48,2,1536]{2,1,0:T(2,128)}, u32[]{:S(2)}) copy-start(f32[48,2,1536]{2,1,0:T(2,128)} %param.33) | copy-start | bytes 1769476
  584.3 282.0 %copy-start.58 = (f32[48,2,1536]{2,1,0:T(2,128)S(1)}, f32[48,2,1536]{2,1,0:T(2,128)}, u32[]{:S(2)}) copy-start(f32[48,2,1536]{2,1,0:T(2,128)} %param.28) | copy-start | bytes 1769476
  681.5 186.3 %copy-start.90 = (f32[48,2]{0,1:T(2,128)}, f32[48,2]{0,1:T(2,128)S(1)}, u32[]{:S(2)}) copy-start(f32[48,2]{0,1:T(2,128)S(1)} %copy.192) | copy-start | bytes 1156
  (82 other events, 420.9 us)
Sparse Core Ops, SparseCore 0:
  10.9 45.0 all-gather.6
  113.5 49.9 all-reduce.12
  166.4 53.1 all-gather.8
  237.9 74.1 reduce-scatter.15
  314.8 41.4 all-gather.10
  367.6 58.9 all-reduce.10
  503.6 55.4 all-reduce.8
  563.2 58.1 reduce-scatter.11
  625.5 55.0 reduce-scatter.17
  684.9 67.0 reduce-scatter.9
  756.2 110.0 reduce-scatter.13
